TPU v7x, 256 devices: a whole 4x4x8 slice. The times are simulated.
256 devices in a mesh: dom: 32 (over x, z), grp: 8 (over y, core).
Axes of the slice: x: 4, y: 4, z: 8, core: 2. Of those that a mesh axis runs over, the one named last changes fastest.
Arguments:
- node_feats: bfloat16 [65536, 1024], P(('dom', 'grp')), may hold values from -6 to 6
- weight: bfloat16 [1024, 512], replicated, may hold values from -0.1875 to 0.1875
- bias: float32 [512], replicated, may hold values from -4 to 4
- cotangent: bfloat16 [65536, 512], P(('dom', 'grp')), may hold values from -6 to 6
- tile_bank: bfloat16 [16, 128, 128], replicated, may hold values from -0.125 to 0.125
- local_cols: int32 [32, 16, 16], P('dom'), may hold values from 0 to 15
- local_banks: int32 [32, 16, 16], P('dom'), may hold values from 0 to 15
- published: int32 [32, 4], P('dom'), may hold values from 0 to 15, as said below
- send_table: int32 [32, 32, 2], replicated, may hold values from -1 to 3, as said below
- halo_rows: int32 [32, 32, 2], P('dom'), may hold values from 0 to 15
- halo_banks: int32 [32, 32, 2], P('dom'), may hold values from 0 to 15
Outputs:
- activations: bfloat16 [65536, 512], P(('dom', 'grp'))
- grad_nodes: bfloat16 [65536, 1024], P(('dom', 'grp'))
- grad_weight: float32 [1024, 512], replicated
- grad_bias: float32 [512], replicated
Inputs may be any that keep to these rules, and one draw needn't show every extreme that they name: `published`: the 4 entries of a partition are distinct block numbers of that partition; 0 and 15 each appear in some partition's list. `send_table`: entry s of the pair (src, p) is -1 or an index into the offered list of src; the live entries of a pair come first and are distinct; a pair (p, p) has none; some pair has all 2 entries live.
All inputs are finite; a program needn't handle non-finite values.
Results may differ from a plain program's by a relative error of at most 0.019.
The roundings to bfloat16 on the way count: a program that leaves them out, or rounds other values in their place, can miss the bound.
Values may be sent and summed in bfloat16 or wider, within the bound.
A program may use at most 64 MiB of HBM per device.

v0:
```python
import jax
import jax.numpy as jnp
from jax import lax
from jax.sharding import PartitionSpec as P


def per_device(
    node_feats,
    weight,
    bias,
    cotangent,
    tile_bank,
    local_cols,
    local_banks,
    published,
    send_table,
    halo_rows,
    halo_banks,
):
    domains = lax.axis_size("dom")
    groups = lax.axis_size("grp")
    domain_index = lax.axis_index("dom")
    rows_here = node_feats.shape[0]
    tile_size = tile_bank.shape[1]
    slot_count = send_table.shape[2]
    pub_count = published.shape[1]
    tiles_row = local_cols.shape[2]
    features = lax.all_to_all(node_feats, "grp", split_axis=1, concat_axis=0, tiled=True)
    part_rows, narrow = features.shape
    blocks = part_rows // tile_size
    feat_blocks = features.reshape(blocks, tile_size, narrow)
    cols_here = local_cols[0]
    banks_here = local_banks[0]
    own_pub = published[0]
    incoming = lax.dynamic_index_in_dim(send_table, domain_index, 1, keepdims=False)
    live_in = (incoming >= 0).astype(jnp.float32)[:, :, None, None]
    rows_in = halo_rows[0]
    halo_tiles = tile_bank[halo_banks[0]]
    source_ids = lax.broadcasted_iota(jnp.int32, (domains, slot_count), 0)
    gathered_ids = source_ids * pub_count + jnp.maximum(incoming, 0)

    def forward_tiles(position, running):
        column = lax.dynamic_index_in_dim(cols_here, position, 1, keepdims=False)
        bank_ids = lax.dynamic_index_in_dim(banks_here, position, 1, keepdims=False)
        return running + jnp.einsum(
            "rij,rjf->rif",
            tile_bank[bank_ids],
            feat_blocks[column],
            preferred_element_type=jnp.float32,
        )

    running = lax.fori_loop(
        0, tiles_row, forward_tiles, jnp.zeros((blocks, tile_size, narrow), jnp.float32)
    )
    shared = feat_blocks[own_pub]
    everyone = lax.all_gather(shared, "dom", axis=0, tiled=True)
    remote = everyone[gathered_ids]
    halo_terms = (
        jnp.einsum("dsij,dsjf->dsif", halo_tiles, remote, preferred_element_type=jnp.float32)
        * live_in
    )
    running = running + jax.ops.segment_sum(
        halo_terms.reshape(domains * slot_count, tile_size, narrow),
        rows_in.reshape(-1),
        num_segments=blocks,
    )
    agg_narrow = running.astype(jnp.bfloat16).reshape(part_rows, narrow)
    aggregated = lax.all_to_all(agg_narrow, "grp", split_axis=0, concat_axis=1, tiled=True)
    pre_act = jnp.dot(aggregated, weight, preferred_element_type=jnp.float32) + bias
    activations = jnp.maximum(pre_act, 0.0).astype(jnp.bfloat16)
    grad_pre = jnp.where(pre_act > 0, cotangent.astype(jnp.float32), 0.0).astype(jnp.bfloat16)
    weight_part = lax.dot_general(
        aggregated, grad_pre, (((0,), (0,)), ((), ())), preferred_element_type=jnp.float32
    )
    bias_part = jnp.sum(grad_pre.astype(jnp.float32), axis=0)
    grad_agg = lax.dot_general(
        grad_pre, weight, (((1,), (1,)), ((), ())), preferred_element_type=jnp.float32
    ).astype(jnp.bfloat16)
    grad_narrow = lax.all_to_all(grad_agg, "grp", split_axis=1, concat_axis=0, tiled=True)
    grad_blocks = grad_narrow.reshape(blocks, tile_size, narrow)

    def backward_tiles(position, running):
        column = lax.dynamic_index_in_dim(cols_here, position, 1, keepdims=False)
        bank_ids = lax.dynamic_index_in_dim(banks_here, position, 1, keepdims=False)
        contrib = jnp.einsum(
            "rji,rjf->rif", tile_bank[bank_ids], grad_blocks, preferred_element_type=jnp.float32
        )
        return running + jax.ops.segment_sum(contrib, column, num_segments=blocks)

    grad_total = lax.fori_loop(
        0, tiles_row, backward_tiles, jnp.zeros((blocks, tile_size, narrow), jnp.float32)
    )
    back_terms = (
        jnp.einsum(
            "dsji,dsjf->dsif", halo_tiles, grad_blocks[rows_in], preferred_element_type=jnp.float32
        )
        * live_in
    )
    placed = jax.ops.segment_sum(
        back_terms.reshape(domains * slot_count, tile_size, narrow),
        gathered_ids.reshape(-1),
        num_segments=domains * pub_count,
    )
    mine_back = lax.psum_scatter(placed, "dom", scatter_dimension=0, tiled=True)
    back_total = jax.ops.segment_sum(mine_back, own_pub, num_segments=blocks)
    grad_total = grad_total + back_total
    grad_nodes = lax.all_to_all(
        grad_total.astype(jnp.bfloat16).reshape(part_rows, narrow),
        "grp",
        split_axis=0,
        concat_axis=1,
        tiled=True,
    )
    norm_scale = float(rows_here * groups * domains) ** (-0.5)
    weight_total, bias_total = lax.psum((weight_part, bias_part), ("dom", "grp"))
    return (activations, grad_nodes, weight_total * norm_scale, bias_total * norm_scale)


def solution(mesh):
    in_specs = (
        P(("dom", "grp"), None),
        P(),
        P(),
        P(("dom", "grp"), None),
        P(),
        P("dom", None, None),
        P("dom", None, None),
        P("dom", None),
        P(),
        P("dom", None, None),
        P("dom", None, None),
    )
    out_specs = (P(("dom", "grp"), None), P(("dom", "grp"), None), P(), P())
    return jax.shard_map(
        per_device, mesh=mesh, in_specs=in_specs, out_specs=out_specs, check_vma=False
    )
```

profile of v0, /device:TPU:2, one launch (start us, length us, event | category | flops | bytes accessed | tf_op | source)
XLA Modules:
  0.0 686.9 jit_solution(15913844381797116386)
XLA Ops:
  9.3 4.5 all-to-all-start
  17.1 7.1 %all-to-all-done = bf16[256,8,128]{2,0,1:T(8,128)(2,1)} async-done(((bf16[256,8,128]{2,0,1:T(8,128)(2,1)}), bf16[256,8,128]{2,0,1:T(8,128)(2,1)}, u32[]{:S(2)}, u32[]{:S(2)}) %all-to-all-start) | async-done | bytes 524320 | tf_op jit(solution)/shard_map/all_to_all | solution.py:28
  26.5 74.0 %while.28 = (s32[]{:T(128)}, f32[16,128,128]{2,1,0:T(8,128)S(1)}, s32[16,16]{0,1:T(8,128)S(1)}, bf16[16,128,128]{2,1,0:T(8,128)(2,1)S(1)}, s32[16,16]{0,1:T(8,12...) while((s32[]{:T(128)}, f32[16,128,128]{2,1,0:T(8,128)S(1)}, ...), condition=%wide.region_1.2_spmd.clone, body=%wide.region_0.1_spmd.clone.sunk | while | flops 67635296 | bytes 5251683 | solution.py:52
  100.5 7.6 %all-gather.3.cloned.1.call-done = bf16[128,128,128]{2,1,0:T(8,128)(2,1)} async-done(((bf16[4,128,128]{2,1,0:T(8,128)(2,1)}), bf16[128,128,128]{2,1,0:T(8,128)(2,1)}) %all-gather.3.cloned.1.call-update) | async-done | bytes 4194320 | tf_op jit(solution)/shard_map/all_gather | solution.py:56
  108.1 4.3 gather_fusion.5
  112.4 4.9 convolution_multiply_fusion.1
  117.2 8.8 %scatter_fusion.1 = f32[16,128,128]{2,1,0:T(8,128)S(1)} fusion(f32[16,128,128]{2,1,0:T(8,128)S(1)} %get-tuple-element.222, s32[64]{0:T(128)S(1)} %reshape.272, f32[64,128,128]{2,1,0:T(8,128)} %bitcast.94), kind=kCustom, calls=%fused_computation.8 | custom fusion | flops 1048576 | bytes 12583168 | tf_op jit(solution)/shard_map/scatter-add | solution.py:62
  126.9 4.4 all-to-all-start.1
  131.6 10.1 %all-to-all-done.1 = bf16[8,256,128]{2,1,0:T(8,128)(2,1)S(1)} async-done(((bf16[8,256,128]{2,1,0:T(8,128)(2,1)}), bf16[8,256,128]{2,1,0:T(8,128)(2,1)S(1)}, u32[]{:S(2)}, u32[]{:S(2)}) %all-to-all-start.1) | async-done | bytes 524320 | tf_op jit(solution)/shard_map/all_to_all | solution.py:68
  144.6 3.5 all-to-all-start.2
  148.6 9.8 %all-to-all-done.2 = bf16[256,8,128]{2,0,1:T(8,128)(2,1)S(1)} async-done(((bf16[256,8,128]{2,0,1:T(8,128)(2,1)}), bf16[256,8,128]{2,0,1:T(8,128)(2,1)S(1)}, u32[]{:S(2)}, u32[]{:S(2)}) %all-to-all-start.2) | async-done | bytes 524320 | tf_op jit(solution)/shard_map/all_to_all | solution.py:79
  160.5 5.2 convolution_multiply_fusion
  165.8 4.3 broadcast_in_dim.12
  170.0 13.4 %scatter_fusion.2 = f32[128,128,128]{2,1,0:T(8,128)} fusion(f32[128,128,128]{2,1,0:T(8,128)} %broadcast_in_dim.12, s32[64]{0:T(128)S(1)} %add_bitcast_fusion, f32[64,128,128]{2,1,0:T(8,128)} %bitcast.93), kind=kCustom, calls=%fused_computation.9 | custom fusion | flops 1048576 | bytes 12583168 | tf_op jit(solution)/shard_map/scatter-add | solution.py:99
  183.5 75.8 %psum.15 = f32[512]{0:T(512)S(1)} all-reduce(f32[512]{0:T(512)S(1)} %get-tuple-element.277), channel_id=1, replica_groups=mesh['dom'=32,'grp'=8] {'dom','grp'}, use_global_device_ids=true, to_apply=%region_11.12 | all-reduce | flops 512 | bytes 4096 | tf_op jit(solution)/shard_map/psum | solution.py:115
  262.2 98.2 %while.27 = (s32[]{:T(128)}, f32[16,128,128]{2,1,0:T(8,128)}, s32[16,16]{0,1:T(8,128)S(1)}, s32[16,16]{0,1:T(8,128)S(1)}, bf16[16,128,128]{2,1,0:T(8,128)(2,1)S(...) while((s32[]{:T(128)}, f32[16,128,128]{2,1,0:T(8,128)}, s32[16,16]{0,1:T(8,128)S(1)}, ...), condition=%wide.region_5.6_spmd, body=%wide.region_3.5_spmd.sunk | while | flops 67372080 | bytes 6296081 | solution.py:90
  265.0 3.3 scatter_fusion
  283.4 3.3 scatter_fusion
  289.6 3.3 scatter_fusion
  301.9 3.3 scatter_fusion
  320.3 3.4 scatter_fusion
  360.4 48.2 %reduce-scatter.2.cloned.1.call-done = f32[4,128,128]{2,1,0:T(8,128)} async-done(((f32[128,128,128]{2,1,0:T(8,128)}), f32[4,128,128]{2,1,0:T(8,128)}) %reduce-scatter.2.cloned.1.call-update) | async-done | bytes 262160 | tf_op jit(solution)/shard_map/reduce_scatter | solution.py:104
  413.3 4.3 all-to-all-start.3
  418.1 257.9 %all-reduce.2.cloned.1.call-done = f32[1024,512]{1,0:T(8,128)} async-done(((f32[1024,512]{1,0:T(8,128)}), f32[1024,512]{1,0:T(8,128)}) %all-reduce.2.cloned.1.call-update) | async-done | bytes 2097168 | tf_op jit(solution)/shard_map/psum | solution.py:115
  (246 shorter events, 181.0 us)
Async XLA Ops:
  7.2 134.8 %copy-start = (bf16[1024,512]{1,0:T(8,128)(2,1)S(1)}, bf16[1024,512]{1,0:T(8,128)(2,1)}, u32[]{:S(2)}) copy-start(bf16[1024,512]{1,0:T(8,128)(2,1)} %param.16) | copy-start | bytes 3145732
  7.2 6.6 copy-start.3
  7.2 6.8 copy-start.8
  7.2 7.4 %copy-start.4 = (s32[1,16,16]{2,1,0:T(8,128)S(1)}, s32[1,16,16]{2,1,0:T(8,128)}, u32[]{:S(2)}) copy-start(s32[1,16,16]{2,1,0:T(8,128)} %param.21) | copy-start | bytes 3076
  7.2 7.4 %copy-start.5 = (s32[1,16,16]{2,1,0:T(8,128)S(1)}, s32[1,16,16]{2,1,0:T(8,128)}, u32[]{:S(2)}) copy-start(s32[1,16,16]{2,1,0:T(8,128)} %param.20) | copy-start | bytes 3076
  7.2 7.5 %copy-start.6 = (s32[1,32,2]{1,2,0:T(2,128)S(1)}, s32[1,32,2]{1,2,0:T(2,128)}, u32[]{:S(2)}) copy-start(s32[1,32,2]{1,2,0:T(2,128)} %param.24) | copy-start | bytes 772
  7.2 7.7 %copy-start.1 = (bf16[16,128,128]{2,1,0:T(8,128)(2,1)S(1)}, bf16[16,128,128]{2,1,0:T(8,128)(2,1)}, u32[]{:S(2)}) copy-start(bf16[16,128,128]{2,1,0:T(8,128)(2,1)} %param.19) | copy-start | bytes 1572868
  9.3 14.9 %all-to-all-start = ((bf16[256,8,128]{2,0,1:T(8,128)(2,1)}), bf16[256,8,128]{2,0,1:T(8,128)(2,1)}, u32[]{:S(2)}, u32[]{:S(2)}) async-start(bf16[256,8,128]{2,0,1:T(8,128)(2,1)} %copy_bitcast_fusion.1), calls=%async_computation | async-start | bytes 1048576 | tf_op jit(solution)/shard_map/all_to_all | solution.py:28
  13.8 94.3 %all-gather.3.cloned.1.call-start = ((), (), s32[]{:S(2)}) async-start(), calls=%async_computation.7 | async-start | bytes 4325376 | tf_op jit(solution)/shard_map/all_gather | solution.py:56
  14.9 2.2 copy-start.9
  126.0 15.9 %copy-start.7 = (f32[512]{0:T(512)S(1)}, f32[512]{0:T(512)}, u32[]{:S(2)}) copy-start(f32[512]{0:T(512)} %param.17) | copy-start | bytes 6148
  126.9 16.2 %copy-start.2 = (bf16[256,512]{1,0:T(8,128)(2,1)S(1)}, bf16[256,512]{1,0:T(8,128)(2,1)}, u32[]{:S(2)}) copy-start(bf16[256,512]{1,0:T(8,128)(2,1)} %param.18) | copy-start | bytes 786436
  126.9 14.8 %all-to-all-start.1 = ((bf16[8,256,128]{2,1,0:T(8,128)(2,1)}), bf16[8,256,128]{2,1,0:T(8,128)(2,1)S(1)}, u32[]{:S(2)}, u32[]{:S(2)}) async-start(bf16[8,256,128]{2,1,0:T(8,128)(2,1)} %bitcast.15), calls=%async_computation.1 | async-start | bytes 1048576 | tf_op jit(solution)/shard_map/all_to_all | solution.py:68
  144.6 13.8 %all-to-all-start.2 = ((bf16[256,8,128]{2,0,1:T(8,128)(2,1)}), bf16[256,8,128]{2,0,1:T(8,128)(2,1)S(1)}, u32[]{:S(2)}, u32[]{:S(2)}) async-start(bf16[256,8,128]{2,0,1:T(8,128)(2,1)} %bitcast.76), calls=%async_computation.2 | async-start | bytes 1048576 | tf_op jit(solution)/shard_map/all_to_all | solution.py:79
  148.1 260.6 %reduce-scatter.2.cloned.1.call-start = ((), (), s32[]{:S(2)}) async-start(), calls=%async_computation.5 | async-start | bytes 8650752 | tf_op jit(solution)/shard_map/reduce_scatter | solution.py:104
  183.5 492.5 %all-reduce.2.cloned.1.call-start = ((), (), s32[]{:S(2)}) async-start(), calls=%async_computation.6 | async-start | bytes 4194304 | tf_op jit(solution)/shard_map/psum | solution.py:115
  413.3 265.9 %all-to-all-start.3 = ((bf16[8,256,128]{2,1,0:T(8,128)(2,1)}), bf16[8,256,128]{2,1,0:T(8,128)(2,1)S(1)}, u32[]{:S(2)}, u32[]{:S(2)}) async-start(bf16[8,256,128]{2,1,0:T(8,128)(2,1)} %bitcast.26), calls=%async_computation.4 | async-start | bytes 1048576 | tf_op jit(solution)/shard_map/all_to_all | solution.py:107
Sparse Core Ops, SparseCore 0:
  26.6 81.3 all-gather.2
  183.6 225.0 reduce-scatter.1
  415.5 260.4 all-reduce.1
where the time goes:
time: 691 us; the launch traced here: 687 us
  waiting for transfers between devices  341 us (49%)
  local copies, waits for them, and re-layouts  94.3 us (14%)
  other arithmetic  85.3 us (12%)
  blocking collectives  75.8 us (11%)
  matrix products  58.9 us (9%)
  starting transfers between devices  16.8 us (2%)
  between operations  14 us (2%)
    psum x1, waiting for transfers between devices, per_device(): lax.psum((weight_part, bias_part), ('dom', 'grp'))  258 us
    psum x1, blocking collectives, per_device(): lax.psum((weight_part, bias_part), ('dom', 'grp'))  75.8 us
    scatter-add x16, other arithmetic, backward_tiles(): return running + jax.ops.segment_sum(contrib, column, num_segments=blocks)  53.1 us
    reduce_scatter x1, waiting for transfers between devices, per_device(): mine_back = lax.psum_scatter(placed, 'dom', scatter_dimension=0, tiled=True)  48.2 us
    gather x16, local copies, waits for them, and re-layouts, forward_tiles(): feat_blocks[column]  39.2 us
    dot_general x16, matrix products, forward_tiles(): jnp.einsum('rij,rjf->rif', tile_bank[bank_ids], feat_blocks[column], pref...  23.2 us
    gather x16, local copies, waits for them, and re-layouts, backward_tiles(): tile_bank[bank_ids]  22.5 us
    dot_general x16, matrix products, backward_tiles(): jnp.einsum('rji,rjf->rif', tile_bank[bank_ids], grad_blocks, preferred_el...  22.3 us
  transfers between devices with their start and end apart: 7, of which 6 were waited for; matrix products, arithmetic and copies ran while one was open for 27% of the time, Pallas kernels for 0%

commit v1 on v0

--- a/solution.py
+++ b/solution.py
@@ -112,7 +112,7 @@
         tiled=True,
     )
     norm_scale = float(rows_here * groups * domains) ** (-0.5)
-    weight_total, bias_total = lax.psum((weight_part, bias_part), ("dom", "grp"))
+    weight_total, bias_total = lax.psum(lax.psum((weight_part, bias_part), "dom"), "grp")
     return (activations, grad_nodes, weight_total * norm_scale, bias_total * norm_scale)
 
 

time: 691 us -> 614 us (0.89)
  waiting for transfers between devices: 341 us -> 254 us
  blocking collectives: 75.8 us -> 91 us
    psum x1 -> x2, waiting for transfers between devices: 258 us -> 97.5 us  [the longest x1 64.7 us: per_device(): lax.psum(lax.psum((weight_part, bias_part), 'dom'), 'grp')]
    reduce_scatter x1, waiting for transfers between devices: 48.2 us -> 132 us  [per_device(): mine_back = lax.psum_scatter(placed, 'dom', scatter_dimension=0, tiled=True)]
    all_to_all x0 -> x1, blocking collectives: none -> 14.6 us  [per_device(): lax.all_to_all(agg_narrow, 'grp', split_axis=0, concat_axis=1, tiled=True)]
    all_to_all x1 -> x0, waiting for transfers between devices: 10.1 us -> none  [per_device(): lax.all_to_all(agg_narrow, 'grp', split_axis=0, concat_axis=1, tiled=True)]
    psum x1 -> x2, blocking collectives: 75.8 us -> 76.4 us  [the longest x1 63.9 us: per_device(): lax.psum((weight_part, bias_part), 'dom')]
  transfers between devices with their start and end apart: 7 -> 7, of which waited for: 6 -> 6; matrix products, arithmetic and copies ran while one was open for 27% -> 34% of each run, Pallas kernels for 0% -> 0%
where the time goes in v1:
time: 614 us; the launch traced here: 610 us
  waiting for transfers between devices  254 us (41%)
  local copies, waits for them, and re-layouts  94.2 us (15%)
  blocking collectives  91 us (15%)
  other arithmetic  84.1 us (14%)
  matrix products  59 us (10%)
  between operations  14.1 us (2%)
  starting transfers between devices  12.4 us (2%)
    reduce_scatter x1, waiting for transfers between devices, per_device(): mine_back = lax.psum_scatter(placed, 'dom', scatter_dimension=0, tiled=True)  132 us
    psum x1, waiting for transfers between devices, per_device(): lax.psum(lax.psum((weight_part, bias_part), 'dom'), 'grp')  64.7 us
    psum x1, blocking collectives, per_device(): lax.psum((weight_part, bias_part), 'dom')  63.9 us
    scatter-add x16, other arithmetic, backward_tiles(): return running + jax.ops.segment_sum(contrib, column, num_segments=blocks)  52.7 us
    gather x16, local copies, waits for them, and re-layouts, forward_tiles(): feat_blocks[column]  39.2 us
    psum x1, waiting for transfers between devices, per_device(): lax.psum((weight_part, bias_part), 'dom')  32.8 us
    dot_general x16, matrix products, forward_tiles(): jnp.einsum('rij,rjf->rif', tile_bank[bank_ids], feat_blocks[column], pref...  23.2 us
    gather x16, local copies, waits for them, and re-layouts, backward_tiles(): tile_bank[bank_ids]  22.5 us
  transfers between devices with their start and end apart: 7, of which 6 were waited for; matrix products, arithmetic and copies ran while one was open for 34% of the time, Pallas kernels for 0%

profile of v1, /device:TPU:2, one launch (start us, length us, event | category | flops | bytes accessed | tf_op | source)
XLA Modules:
  0.0 610.0 jit_solution(2101844328220292870)
XLA Ops:
  9.3 4.5 all-to-all-start
  17.1 7.1 %all-to-all-done = bf16[256,8,128]{2,0,1:T(8,128)(2,1)} async-done(((bf16[256,8,128]{2,0,1:T(8,128)(2,1)}), bf16[256,8,128]{2,0,1:T(8,128)(2,1)}, u32[]{:S(2)}, u32[]{:S(2)}) %all-to-all-start) | async-done | bytes 524320 | tf_op jit(solution)/shard_map/all_to_all | solution.py:28
  26.5 74.0 %while.28 = (s32[]{:T(128)}, f32[16,128,128]{2,1,0:T(8,128)S(1)}, s32[16,16]{0,1:T(8,128)S(1)}, bf16[16,128,128]{2,1,0:T(8,128)(2,1)S(1)}, s32[16,16]{0,1:T(8,12...) while((s32[]{:T(128)}, f32[16,128,128]{2,1,0:T(8,128)S(1)}, ...), condition=%wide.region_1.2_spmd.clone, body=%wide.region_0.1_spmd.clone.sunk | while | flops 67635296 | bytes 5251683 | solution.py:52
  100.5 7.5 %all-gather.3.cloned.1.call-done = bf16[128,128,128]{2,1,0:T(8,128)(2,1)} async-done(((bf16[4,128,128]{2,1,0:T(8,128)(2,1)}), bf16[128,128,128]{2,1,0:T(8,128)(2,1)}) %all-gather.3.cloned.1.call-update) | async-done | bytes 4194320 | tf_op jit(solution)/shard_map/all_gather | solution.py:56
  108.1 4.3 gather_fusion.5
  112.4 4.9 convolution_multiply_fusion.1
  117.2 8.8 %scatter_fusion.1 = f32[16,128,128]{2,1,0:T(8,128)S(1)} fusion(f32[16,128,128]{2,1,0:T(8,128)S(1)} %get-tuple-element.222, s32[64]{0:T(128)S(1)} %reshape.272, f32[64,128,128]{2,1,0:T(8,128)} %bitcast.94), kind=kCustom, calls=%fused_computation.8 | custom fusion | flops 1048576 | bytes 12583168 | tf_op jit(solution)/shard_map/scatter-add | solution.py:62
  126.2 14.6 %all_to_all.70 = bf16[8,256,128]{2,1,0:T(8,128)(2,1)S(1)} all-to-all(bf16[8,256,128]{2,1,0:T(8,128)(2,1)S(1)} %bitcast.99), channel_id=1, replica_groups=mesh['dom'=32,'grp'=8] {'grp'}, dimensions={0} | all-to-all | bytes 1048576 | tf_op jit(solution)/shard_map/all_to_all | solution.py:68
  145.6 3.5 all-to-all-start.2
  149.6 9.8 %all-to-all-done.2 = bf16[256,8,128]{2,0,1:T(8,128)(2,1)S(1)} async-done(((bf16[256,8,128]{2,0,1:T(8,128)(2,1)}), bf16[256,8,128]{2,0,1:T(8,128)(2,1)S(1)}, u32[]{:S(2)}, u32[]{:S(2)}) %all-to-all-start.2) | async-done | bytes 524320 | tf_op jit(solution)/shard_map/all_to_all | solution.py:79
  161.6 5.3 convolution_multiply_fusion
  166.8 4.3 broadcast_in_dim.12
  171.1 13.4 %scatter_fusion.2 = f32[128,128,128]{2,1,0:T(8,128)} fusion(f32[128,128,128]{2,1,0:T(8,128)} %broadcast_in_dim.12, s32[64]{0:T(128)S(1)} %add_bitcast_fusion, f32[64,128,128]{2,1,0:T(8,128)} %bitcast.93), kind=kCustom, calls=%fused_computation.9 | custom fusion | flops 1048576 | bytes 12583168 | tf_op jit(solution)/shard_map/scatter-add | solution.py:99
  184.6 63.9 %psum.30 = f32[512]{0:T(512)S(1)} all-reduce(f32[512]{0:T(512)S(1)} %get-tuple-element.277), channel_id=1, replica_groups=mesh['dom'=32,'grp'=8] {'dom'}, use_global_device_ids=true, to_apply=%region_12.13 | all-reduce | flops 512 | bytes 4096 | tf_op jit(solution)/shard_map/psum | solution.py:115
  248.5 12.4 %psum.31 = f32[512]{0:T(512)S(1)} all-reduce(f32[512]{0:T(512)S(1)} %psum.30), channel_id=1, replica_groups=mesh['dom'=32,'grp'=8] {'grp'}, use_global_device_ids=true, to_apply=%region_13.14 | all-reduce | flops 512 | bytes 4096 | tf_op jit(solution)/shard_map/psum | solution.py:115
  261.0 32.8 %all-reduce.3.cloned.1.call-done = f32[1024,512]{1,0:T(8,128)} async-done(((f32[1024,512]{1,0:T(8,128)}), f32[1024,512]{1,0:T(8,128)}) %all-reduce.3.cloned.1.call-update) | async-done | bytes 2097168 | tf_op jit(solution)/shard_map/psum | solution.py:115
  294.8 97.9 %while.27 = (s32[]{:T(128)}, f32[16,128,128]{2,1,0:T(8,128)}, s32[16,16]{0,1:T(8,128)S(1)}, s32[16,16]{0,1:T(8,128)S(1)}, bf16[16,128,128]{2,1,0:T(8,128)(2,1)S(...) while((s32[]{:T(128)}, f32[16,128,128]{2,1,0:T(8,128)}, s32[16,16]{0,1:T(8,128)S(1)}, ...), condition=%wide.region_5.6_spmd, body=%wide.region_3.5_spmd.sunk | while | flops 67372080 | bytes 6296081 | solution.py:90
  322.1 3.3 scatter_fusion
  340.4 3.3 scatter_fusion
  352.7 3.3 scatter_fusion
  389.4 3.3 scatter_fusion
  392.7 132.2 %reduce-scatter.2.cloned.1.call-done = f32[4,128,128]{2,1,0:T(8,128)} async-done(((f32[128,128,128]{2,1,0:T(8,128)}), f32[4,128,128]{2,1,0:T(8,128)}) %reduce-scatter.2.cloned.1.call-update) | async-done | bytes 262160 | tf_op jit(solution)/shard_map/reduce_scatter | solution.py:104
  529.5 4.3 all-to-all-start.3
  534.4 64.7 %all-reduce.5.cloned.1.call-done = f32[1024,512]{1,0:T(8,128)} async-done(((f32[1024,512]{1,0:T(8,128)}), f32[1024,512]{1,0:T(8,128)}) %all-reduce.5.cloned.1.call-update) | async-done | bytes 2097168 | tf_op jit(solution)/shard_map/psum | solution.py:115
  (249 shorter events, 183.3 us)
Async XLA Ops:
  7.2 133.8 %copy-start = (bf16[1024,512]{1,0:T(8,128)(2,1)S(1)}, bf16[1024,512]{1,0:T(8,128)(2,1)}, u32[]{:S(2)}) copy-start(bf16[1024,512]{1,0:T(8,128)(2,1)} %param.16) | copy-start | bytes 3145732
  7.2 6.6 %copy-start.3 = (s32[32,32,2]{1,2,0:T(2,128)S(1)}, s32[32,32,2]{1,2,0:T(2,128)}, u32[]{:S(2)}) copy-start(s32[32,32,2]{1,2,0:T(2,128)} %param.23) | copy-start | bytes 24580
  7.2 6.8 %copy-start.8 = (s32[1,32,2]{1,2,0:T(2,128)S(1)}, s32[1,32,2]{1,2,0:T(2,128)}, u32[]{:S(2)}) copy-start(s32[1,32,2]{1,2,0:T(2,128)} %param.25) | copy-start | bytes 772
  7.2 7.4 %copy-start.4 = (s32[1,16,16]{2,1,0:T(8,128)S(1)}, s32[1,16,16]{2,1,0:T(8,128)}, u32[]{:S(2)}) copy-start(s32[1,16,16]{2,1,0:T(8,128)} %param.21) | copy-start | bytes 3076
  7.2 7.4 %copy-start.5 = (s32[1,16,16]{2,1,0:T(8,128)S(1)}, s32[1,16,16]{2,1,0:T(8,128)}, u32[]{:S(2)}) copy-start(s32[1,16,16]{2,1,0:T(8,128)} %param.20) | copy-start | bytes 3076
  7.2 7.5 %copy-start.6 = (s32[1,32,2]{1,2,0:T(2,128)S(1)}, s32[1,32,2]{1,2,0:T(2,128)}, u32[]{:S(2)}) copy-start(s32[1,32,2]{1,2,0:T(2,128)} %param.24) | copy-start | bytes 772
  7.2 7.7 %copy-start.1 = (bf16[16,128,128]{2,1,0:T(8,128)(2,1)S(1)}, bf16[16,128,128]{2,1,0:T(8,128)(2,1)}, u32[]{:S(2)}) copy-start(bf16[16,128,128]{2,1,0:T(8,128)(2,1)} %param.19) | copy-start | bytes 1572868
  9.3 14.9 %all-to-all-start = ((bf16[256,8,128]{2,0,1:T(8,128)(2,1)}), bf16[256,8,128]{2,0,1:T(8,128)(2,1)}, u32[]{:S(2)}, u32[]{:S(2)}) async-start(bf16[256,8,128]{2,0,1:T(8,128)(2,1)} %copy_bitcast_fusion.1), calls=%async_computation | async-start | bytes 1048576 | tf_op jit(solution)/shard_map/all_to_all | solution.py:28
  13.8 94.3 %all-gather.3.cloned.1.call-start = ((), (), s32[]{:S(2)}) async-start(), calls=%async_computation.8 | async-start | bytes 4325376 | tf_op jit(solution)/shard_map/all_gather | solution.py:56
  14.9 2.2 copy-start.9
  26.5 267.2 %all-reduce.3.cloned.1.call-start = ((), (), s32[]{:S(2)}) async-start(), calls=%async_computation.6 | async-start | bytes 4194304 | tf_op jit(solution)/shard_map/psum | solution.py:115
  126.0 15.0 %copy-start.7 = (f32[512]{0:T(512)S(1)}, f32[512]{0:T(512)}, u32[]{:S(2)}) copy-start(f32[512]{0:T(512)} %param.17) | copy-start | bytes 6148
  126.1 16.0 %copy-start.2 = (bf16[256,512]{1,0:T(8,128)(2,1)S(1)}, bf16[256,512]{1,0:T(8,128)(2,1)}, u32[]{:S(2)}) copy-start(bf16[256,512]{1,0:T(8,128)(2,1)} %param.18) | copy-start | bytes 786436
  145.6 13.8 %all-to-all-start.2 = ((bf16[256,8,128]{2,0,1:T(8,128)(2,1)}), bf16[256,8,128]{2,0,1:T(8,128)(2,1)S(1)}, u32[]{:S(2)}, u32[]{:S(2)}) async-start(bf16[256,8,128]{2,0,1:T(8,128)(2,1)} %bitcast.76), calls=%async_computation.2 | async-start | bytes 1048576 | tf_op jit(solution)/shard_map/all_to_all | solution.py:79
  149.1 375.8 %reduce-scatter.2.cloned.1.call-start = ((), (), s32[]{:S(2)}) async-start(), calls=%async_computation.5 | async-start | bytes 8650752 | tf_op jit(solution)/shard_map/reduce_scatter | solution.py:104
  184.5 414.6 %all-reduce.5.cloned.1.call-start = ((), (), s32[]{:S(2)}) async-start(), calls=%async_computation.7 | async-start | bytes 4194304 | tf_op jit(solution)/shard_map/psum | solution.py:115
  529.5 72.8 %all-to-all-start.3 = ((bf16[8,256,128]{2,1,0:T(8,128)(2,1)}), bf16[8,256,128]{2,1,0:T(8,128)(2,1)S(1)}, u32[]{:S(2)}, u32[]{:S(2)}) async-start(bf16[8,256,128]{2,1,0:T(8,128)(2,1)} %bitcast.26), calls=%async_computation.4 | async-start | bytes 1048576 | tf_op jit(solution)/shard_map/all_to_all | solution.py:107
Sparse Core Ops, SparseCore 0:
  26.6 81.3 all-gather.2
  144.2 149.4 all-reduce.2
  298.3 226.5 reduce-scatter.1
  527.1 71.9 all-reduce.4
